TPU v7x, 512 devices: a whole 4x4x16 slice. The times are simulated.
512 devices in a mesh: row: 32 (over z, y_lo), col: 16 (over y_hi, x, core).
Axes of the slice: x: 4, y: 4 (y_hi: 2, y_lo: 2; y = y_hi * 2 + y_lo), z: 16, core: 2. Of those that a mesh axis runs over, the one named last changes fastest.
Arguments:
- coords: int32 [3, 65536], P(None, ('row', 'col')), may hold values from 0 to 60809, as said below
- mode_shapes: bfloat16 [256, 65536], P(None, ('row', 'col')), as said below
- output_shapes: bfloat16 [1048576, 256], P(('row', 'col')), may hold values from -0.375 to 0.375
- response_gain: float32 [2, 256], replicated, may hold values from -4 to 4
Outputs:
- response_power: float32 [1048576], P(('row', 'col'))
- modal_csd: float32 [256, 256], replicated
Inputs may be any that keep to these rules, and one draw needn't show every extreme that they name: `coords`: positions of points on an aircraft's skin, numbered in no spatial order. `mode_shapes`: entries are of order 1 / sqrt(65536); each mode has a share of one sign over all nodes.
All inputs are finite; a program needn't handle non-finite values.
Results may differ from a plain program's by a relative error of at most 0.002.
Values may be sent and summed in bfloat16 or wider, within the bound.
A program may use at most 64 MiB of HBM per device.

v0:
```python
import math
import jax
import jax.numpy as jnp
from jax import lax
from jax.sharding import PartitionSpec as P

wave_scale = 0.35 / 64.0


def coherence(left_points, right_points):
    difference = (left_points[:, :, None] - right_points[:, None, :]).astype(jnp.float32)
    squared = jnp.sum(difference * difference, axis=0)
    return jnp.sinc(wave_scale * jnp.sqrt(squared)).astype(jnp.bfloat16)


def split_parts(matrix):
    high_part = matrix.astype(jnp.bfloat16)
    low_part = (matrix - high_part.astype(jnp.float32)).astype(jnp.bfloat16)
    return (high_part, low_part)


def modal_product(node_shapes, node_projection):
    high_part, low_part = split_parts(node_projection)
    dims = (((1,), (1,)), ((), ()))
    upper = lax.dot_general(node_shapes, high_part, dims, preferred_element_type=jnp.float32)
    lower = lax.dot_general(node_shapes, low_part, dims, preferred_element_type=jnp.float32)
    return upper + lower


def local(coords, mode_shapes, output_shapes, response_gain):
    row_shapes, row_points = (
        lax.all_gather(mode_shapes, "col", axis=1, tiled=True),
        lax.all_gather(coords, "col", axis=1, tiled=True),
    )
    mode_count = mode_shapes.shape[0]
    zero_block = jnp.zeros((mode_count, row_points.shape[1]), jnp.float32)
    piece_shapes = lax.all_gather(mode_shapes, "row", axis=1, tiled=True)
    piece_points = lax.all_gather(coords, "row", axis=1, tiled=True)
    length = piece_shapes.shape[1]
    block_size = math.gcd(length, 1024)
    block_count = length // block_size

    def add_block(loop_index, running_sum):
        block_start = loop_index * block_size
        part_shapes = lax.dynamic_slice_in_dim(piece_shapes, block_start, block_size, 1)
        part_points = lax.dynamic_slice_in_dim(piece_points, block_start, block_size, 1)
        coherence_tile = coherence(part_points, row_points)
        return running_sum + jnp.dot(
            part_shapes, coherence_tile, preferred_element_type=jnp.float32
        )

    projection = lax.fori_loop(0, block_count, add_block, zero_block)
    partial_csd = modal_product(row_shapes, projection)
    modal_csd = lax.psum(partial_csd, ("row", "col"))
    real_part = response_gain[0]
    imag_part = response_gain[1]
    weighted = (
        real_part[:, None] * real_part[None, :] + imag_part[:, None] * imag_part[None, :]
    ) * modal_csd
    weighted_high, weighted_low = split_parts(weighted)
    mapped = jnp.dot(output_shapes, weighted_high, preferred_element_type=jnp.float32)
    mapped = mapped + jnp.dot(output_shapes, weighted_low, preferred_element_type=jnp.float32)
    response_power = jnp.sum(mapped * output_shapes.astype(jnp.float32), axis=1)
    return (response_power, modal_csd)


def solution(mesh):
    in_specs = (P(None, ("row", "col")), P(None, ("row", "col")), P(("row", "col"), None), P())
    out_specs = (P(("row", "col")), P())
    return jax.shard_map(local, mesh=mesh, in_specs=in_specs, out_specs=out_specs, check_vma=False)
```

profile of v0, /device:TPU:4, one launch (start us, length us, event | category | flops | bytes accessed | tf_op | source)
XLA Modules:
  0.0 702.3 jit_solution(17819532380165018910)
XLA Ops:
  7.2 0.0 all-gather.3.cloned.1.call-start
  7.2 0.7 all-gather.3.cloned.1.call-update
  7.9 0.0 all-gather.5.cloned.1.call-start
  7.9 0.7 all-gather.5.cloned.1.call-update
  8.6 0.0 all-reduce.2.cloned.1.call-start
  8.7 69.6 %all_gather.13 = s32[3,4096]{1,0:T(4,128)S(1)} all-gather(s32[3,128]{1,0:T(4,128)} %param.6), channel_id=1, replica_groups=mesh['row'=32,'col'=16] {'row'}, dimensions={1}, use_global_device_ids=true | all-gather | bytes 50688 | tf_op jit(solution)/shard_map/all_gather | solution.py:38
  78.3 19.8 %all_gather.14 = s32[3,2048]{1,0:T(4,128)S(1)} all-gather(s32[3,128]{1,0:T(4,128)} %param.6), channel_id=1, replica_groups=mesh['row'=32,'col'=16] {'col'}, dimensions={1}, use_global_device_ids=true | all-gather | bytes 26112 | tf_op jit(solution)/shard_map/all_gather | solution.py:33
  98.1 2.3 copy.8
  100.4 50.3 %all-gather.3.cloned.1.call-done = bf16[256,4096]{1,0:T(8,128)(2,1)} async-done(((bf16[256,128]{1,0:T(8,128)(2,1)}), bf16[256,4096]{1,0:T(8,128)(2,1)}) %all-gather.3.cloned.1.call-update) | async-done | bytes 2097168 | tf_op jit(solution)/shard_map/all_gather | solution.py:37
  150.7 81.9 %while.16 = (s32[]{:T(128)}, f32[256,2048]{1,0:T(8,128)S(1)}, bf16[256,4096]{1,0:T(8,128)(2,1)}, s32[3,4096]{1,0:T(4,128)S(1)}, s32[3,2048]{1,0:T(4,128)S(1)}, /*index=5*/s32[]{:T(128)}, s32[]{:T(128)}, s32[]{:T(128)}, s32[]{:T(128)}) while((s32[]{:T(128)}, f32[256,2048]{1,0:T(8,128)S(1)}, bf16[256,4096]{1,0:T(8,128)(2,1)}, ...), condition=%wide.region_2.3_spmd.clone, body=%wide.region_0.2_spmd.clone.sunk | while | flops 1171259392 | bytes 21557404 | solution.py:52
  150.7 6.3 multiply_reduce_fusion.2
  157.0 14.1 %fusion.60 = f32[256,2048]{1,0:T(8,128)S(1)} fusion(f32[1024,2048]{1,0:T(8,128)} %multiply_reduce_fusion.2, f32[256,2048]{1,0:T(8,128)S(1)} %get-tuple-element.211, pred[]{:T(512)S(6)} %compare.3, bf16[256,4096]{1,0:T(8,128)(2,1)} %get-tuple-element.221, s32[]{:T(128)S(6)} %select_n.137), kind=kOutput, calls=%fused_computation.26.clone.1 | convolution fusion | flops 1148190720 | bytes 13107205 | tf_op jit(solution)/shard_map/while/body/eval_jaxpr/dot_general | solution.py:48
  171.2 6.3 multiply_reduce_fusion.2
  177.5 14.1 %fusion.60 = f32[256,2048]{1,0:T(8,128)S(1)} fusion(f32[1024,2048]{1,0:T(8,128)} %multiply_reduce_fusion.2, f32[256,2048]{1,0:T(8,128)S(1)} %get-tuple-element.211, pred[]{:T(512)S(6)} %compare.3, bf16[256,4096]{1,0:T(8,128)(2,1)} %get-tuple-element.221, s32[]{:T(128)S(6)} %select_n.137), kind=kOutput, calls=%fused_computation.26.clone.1 | convolution fusion | flops 1148190720 | bytes 13107205 | tf_op jit(solution)/shard_map/while/body/eval_jaxpr/dot_general | solution.py:48
  191.7 6.3 multiply_reduce_fusion.2
  198.0 14.1 %fusion.60 = f32[256,2048]{1,0:T(8,128)S(1)} fusion(f32[1024,2048]{1,0:T(8,128)} %multiply_reduce_fusion.2, f32[256,2048]{1,0:T(8,128)S(1)} %get-tuple-element.211, pred[]{:T(512)S(6)} %compare.3, bf16[256,4096]{1,0:T(8,128)(2,1)} %get-tuple-element.221, s32[]{:T(128)S(6)} %select_n.137), kind=kOutput, calls=%fused_computation.26.clone.1 | convolution fusion | flops 1148190720 | bytes 13107205 | tf_op jit(solution)/shard_map/while/body/eval_jaxpr/dot_general | solution.py:48
  212.1 6.3 multiply_reduce_fusion.2
  218.5 14.1 %fusion.60 = f32[256,2048]{1,0:T(8,128)S(1)} fusion(f32[1024,2048]{1,0:T(8,128)} %multiply_reduce_fusion.2, f32[256,2048]{1,0:T(8,128)S(1)} %get-tuple-element.211, pred[]{:T(512)S(6)} %compare.3, bf16[256,4096]{1,0:T(8,128)(2,1)} %get-tuple-element.221, s32[]{:T(128)S(6)} %select_n.137), kind=kOutput, calls=%fused_computation.26.clone.1 | convolution fusion | flops 1148190720 | bytes 13107205 | tf_op jit(solution)/shard_map/while/body/eval_jaxpr/dot_general | solution.py:48
  232.6 1.8 fusion.37
  234.4 2.4 fusion.35
  236.9 453.2 %all-reduce.2.cloned.1.call-done = f32[256,256]{0,1:T(8,128)} async-done(((f32[256,256]{0,1:T(8,128)}), f32[256,256]{0,1:T(8,128)}) %all-reduce.2.cloned.1.call-update) | async-done | bytes 262160 | tf_op jit(solution)/shard_map/psum | solution.py:54
  690.1 1.8 copy.9
  691.9 1.4 fusion.40
  693.3 2.5 fusion.34
  (12 shorter events, 0.1 us)
Async XLA Ops:
  7.2 143.5 %all-gather.3.cloned.1.call-start = ((), (), s32[]{:S(2)}) async-start(), calls=%async_computation | async-start | bytes 2162688 | tf_op jit(solution)/shard_map/all_gather | solution.py:37
  7.9 224.7 %all-gather.5.cloned.1.call-start = ((), (), s32[]{:S(2)}) async-start(), calls=%async_computation.1 | async-start | bytes 1114112 | tf_op jit(solution)/shard_map/all_gather | solution.py:32
  8.6 681.4 %all-reduce.2.cloned.1.call-start = ((), (), s32[]{:S(2)}) async-start(), calls=%async_computation.2 | async-start | bytes 524288 | tf_op jit(solution)/shard_map/psum | solution.py:54
  150.7 86.2 %copy-start.1 = (f32[2,256]{1,0:T(2,128)S(1)}, f32[2,256]{1,0:T(2,128)}, u32[]{:S(2)}) copy-start(f32[2,256]{1,0:T(2,128)} %param.9) | copy-start | bytes 6148
  232.6 459.3 %copy-start = (bf16[2048,256]{1,0:T(8,128)(2,1)S(1)}, bf16[2048,256]{1,0:T(8,128)(2,1)}, u32[]{:S(2)}) copy-start(bf16[2048,256]{1,0:T(8,128)(2,1)} %param.8) | copy-start | bytes 3145732
Sparse Core Ops, SparseCore 0:
  10.0 140.6 all-gather.2
  153.8 55.1 all-gather.4
  237.0 453.0 all-reduce.1
where the time goes:
time: 703 us; the launch traced here: 702 us
  waiting for transfers between devices  505 us (72%)
  blocking collectives  89.4 us (13%)
  matrix products  64.5 us (9%)
  other arithmetic  25.3 us (4%)
  between operations  13.8 us (2%)
    psum x1, waiting for transfers between devices, local(): modal_csd = lax.psum(partial_csd, ('row', 'col'))  453 us
    all_gather x1, blocking collectives, local(): piece_points = lax.all_gather(coords, 'row', axis=1, tiled=True)  69.6 us
    dot_general x4, matrix products, add_block(): jnp.dot(part_shapes, coherence_tile, preferred_element_type=jnp.float32)  56.4 us
    all_gather x1, waiting for transfers between devices, local(): piece_shapes = lax.all_gather(mode_shapes, 'row', axis=1, tiled=True)  50.3 us
    reduce_sum x4, other arithmetic, coherence(): squared = jnp.sum(difference * difference, axis=0)  25.3 us
    all_gather x1, blocking collectives, local(): lax.all_gather(coords, 'col', axis=1, tiled=True)  19.8 us
  transfers between devices with their start and end apart: 3, of which 2 were waited for; matrix products, arithmetic and copies ran while one was open for 12% of the time, Pallas kernels for 0%

commit v1 on v0

--- a/solution.py
+++ b/solution.py
@@ -51,7 +51,9 @@
 
     projection = lax.fori_loop(0, block_count, add_block, zero_block)
     partial_csd = modal_product(row_shapes, projection)
-    modal_csd = lax.psum(partial_csd, ("row", "col"))
+    modal_csd = partial_csd
+    for over in ("col", "row"):
+        modal_csd = lax.psum(modal_csd, over)
     real_part = response_gain[0]
     imag_part = response_gain[1]
     weighted = (

time: 703 us -> 663 us (0.943)
  the two profiles are of different devices: /device:TPU:4 before, /device:TPU:2 now
where the time goes in v1:
time: 663 us
  waiting for transfers between devices  467 us (70%)
  blocking collectives  89.6 us (14%)
  matrix products  64.1 us (10%)
  other arithmetic  25.3 us (4%)
  between operations  13.8 us (2%)
    psum x2, waiting for transfers between devices, local(): modal_csd = lax.psum(modal_csd, over)  413 us
    all_gather x1, blocking collectives, local(): piece_points = lax.all_gather(coords, 'row', axis=1, tiled=True)  69.6 us
    dot_general x4, matrix products, add_block(): jnp.dot(part_shapes, coherence_tile, preferred_element_type=jnp.float32)  56.4 us
    all_gather x1, waiting for transfers between devices, local(): piece_shapes = lax.all_gather(mode_shapes, 'row', axis=1, tiled=True)  52.6 us
    reduce_sum x4, other arithmetic, coherence(): squared = jnp.sum(difference * difference, axis=0)  25.3 us
    all_gather x1, blocking collectives, local(): lax.all_gather(coords, 'col', axis=1, tiled=True)  20 us
  transfers between devices with their start and end apart: 4, of which 3 were waited for; matrix products, arithmetic and copies ran while one was open for 12% of the time, Pallas kernels for 0%

profile of v1, /device:TPU:2, one launch (start us, length us, event | category | flops | bytes accessed | tf_op | source)
XLA Modules:
  0.0 662.8 jit_solution(7352508061694699674)
XLA Ops:
  7.2 0.7 all-gather.3.cloned.1.call-update
  7.9 0.7 all-gather.5.cloned.1.call-update
  8.6 0.0 all-reduce.3.cloned.1.call-start
  8.7 69.6 %all_gather.13 = s32[3,4096]{1,0:T(4,128)S(1)} all-gather(s32[3,128]{1,0:T(4,128)} %param.6), channel_id=1, replica_groups=mesh['row'=32,'col'=16] {'row'}, dimensions={1}, use_global_device_ids=true | all-gather | bytes 50688 | tf_op jit(solution)/shard_map/all_gather | solution.py:38
  78.3 20.0 %all_gather.14 = s32[3,2048]{1,0:T(4,128)S(1)} all-gather(s32[3,128]{1,0:T(4,128)} %param.6), channel_id=1, replica_groups=mesh['row'=32,'col'=16] {'col'}, dimensions={1}, use_global_device_ids=true | all-gather | bytes 26112 | tf_op jit(solution)/shard_map/all_gather | solution.py:33
  98.3 52.6 %all-gather.3.cloned.1.call-done = bf16[256,4096]{1,0:T(8,128)(2,1)} async-done(((bf16[256,128]{1,0:T(8,128)(2,1)}), bf16[256,4096]{1,0:T(8,128)(2,1)}) %all-gather.3.cloned.1.call-update) | async-done | bytes 2097168 | tf_op jit(solution)/shard_map/all_gather | solution.py:37
  150.9 81.9 %while.16 = (s32[]{:T(128)}, f32[256,2048]{1,0:T(8,128)S(1)}, bf16[256,4096]{1,0:T(8,128)(2,1)}, s32[3,4096]{1,0:T(4,128)S(1)}, s32[3,2048]{1,0:T(4,128)S(1)}, /*index=5*/s32[]{:T(128)}, s32[]{:T(128)}, s32[]{:T(128)}, s32[]{:T(128)}) while((s32[]{:T(128)}, f32[256,2048]{1,0:T(8,128)S(1)}, bf16[256,4096]{1,0:T(8,128)(2,1)}, ...), condition=%wide.region_2.3_spmd.clone, body=%wide.region_0.2_spmd.clone.sunk | while | flops 1171259392 | bytes 21557404 | solution.py:52
  150.9 6.3 multiply_reduce_fusion.2
  157.2 14.1 %fusion.60 = f32[256,2048]{1,0:T(8,128)S(1)} fusion(f32[1024,2048]{1,0:T(8,128)} %multiply_reduce_fusion.2, f32[256,2048]{1,0:T(8,128)S(1)} %get-tuple-element.211, pred[]{:T(512)S(6)} %compare.3, bf16[256,4096]{1,0:T(8,128)(2,1)} %get-tuple-element.221, s32[]{:T(128)S(6)} %select_n.137), kind=kOutput, calls=%fused_computation.26.clone.1 | convolution fusion | flops 1148190720 | bytes 13107205 | tf_op jit(solution)/shard_map/while/body/eval_jaxpr/dot_general | solution.py:48
  171.4 6.3 multiply_reduce_fusion.2
  177.7 14.1 %fusion.60 = f32[256,2048]{1,0:T(8,128)S(1)} fusion(f32[1024,2048]{1,0:T(8,128)} %multiply_reduce_fusion.2, f32[256,2048]{1,0:T(8,128)S(1)} %get-tuple-element.211, pred[]{:T(512)S(6)} %compare.3, bf16[256,4096]{1,0:T(8,128)(2,1)} %get-tuple-element.221, s32[]{:T(128)S(6)} %select_n.137), kind=kOutput, calls=%fused_computation.26.clone.1 | convolution fusion | flops 1148190720 | bytes 13107205 | tf_op jit(solution)/shard_map/while/body/eval_jaxpr/dot_general | solution.py:48
  191.9 6.3 multiply_reduce_fusion.2
  198.2 14.1 %fusion.60 = f32[256,2048]{1,0:T(8,128)S(1)} fusion(f32[1024,2048]{1,0:T(8,128)} %multiply_reduce_fusion.2, f32[256,2048]{1,0:T(8,128)S(1)} %get-tuple-element.211, pred[]{:T(512)S(6)} %compare.3, bf16[256,4096]{1,0:T(8,128)(2,1)} %get-tuple-element.221, s32[]{:T(128)S(6)} %select_n.137), kind=kOutput, calls=%fused_computation.26.clone.1 | convolution fusion | flops 1148190720 | bytes 13107205 | tf_op jit(solution)/shard_map/while/body/eval_jaxpr/dot_general | solution.py:48
  212.4 6.3 multiply_reduce_fusion.2
  218.7 14.1 %fusion.60 = f32[256,2048]{1,0:T(8,128)S(1)} fusion(f32[1024,2048]{1,0:T(8,128)} %multiply_reduce_fusion.2, f32[256,2048]{1,0:T(8,128)S(1)} %get-tuple-element.211, pred[]{:T(512)S(6)} %compare.3, bf16[256,4096]{1,0:T(8,128)(2,1)} %get-tuple-element.221, s32[]{:T(128)S(6)} %select_n.137), kind=kOutput, calls=%fused_computation.26.clone.1 | convolution fusion | flops 1148190720 | bytes 13107205 | tf_op jit(solution)/shard_map/while/body/eval_jaxpr/dot_general | solution.py:48
  232.9 1.7 fusion.37
  234.6 2.4 fusion.35
  237.0 0.0 all-reduce.5.cloned.1.call-start
  237.0 144.8 %all-reduce.3.cloned.1.call-done = f32[256,256]{0,1:T(8,128)} async-done(((f32[256,256]{0,1:T(8,128)}), f32[256,256]{0,1:T(8,128)}) %all-reduce.3.cloned.1.call-update) | async-done | bytes 262160 | tf_op jit(solution)/shard_map/psum | solution.py:56
  381.9 0.6 copy.8
  382.6 268.3 %all-reduce.5.cloned.1.call-done = f32[256,256]{0,1:T(8,128)} async-done(((f32[256,256]{0,1:T(8,128)}), f32[256,256]{0,1:T(8,128)}) %all-reduce.5.cloned.1.call-update) | async-done | bytes 262160 | tf_op jit(solution)/shard_map/psum | solution.py:56
  650.9 1.8 copy.9
  652.7 1.4 fusion.40
  654.1 2.1 fusion.34
  (15 shorter events, 0.2 us)
Async XLA Ops:
  7.2 143.7 %all-gather.3.cloned.1.call-start = ((), (), s32[]{:S(2)}) async-start(), calls=%async_computation | async-start | bytes 2162688 | tf_op jit(solution)/shard_map/all_gather | solution.py:37
  7.9 225.0 %all-gather.5.cloned.1.call-start = ((), (), s32[]{:S(2)}) async-start(), calls=%async_computation.1 | async-start | bytes 1114112 | tf_op jit(solution)/shard_map/all_gather | solution.py:32
  8.6 373.2 %all-reduce.3.cloned.1.call-start = ((), (), s32[]{:S(2)}) async-start(), calls=%async_computation.2 | async-start | bytes 524288 | tf_op jit(solution)/shard_map/psum | solution.py:56
  150.9 231.0 %copy-start = (bf16[2048,256]{1,0:T(8,128)(2,1)S(1)}, bf16[2048,256]{1,0:T(8,128)(2,1)}, u32[]{:S(2)}) copy-start(bf16[2048,256]{1,0:T(8,128)(2,1)} %param.8) | copy-start | bytes 3145732
  232.8 149.8 %copy-start.1 = (f32[2,256]{1,0:T(2,128)S(1)}, f32[2,256]{1,0:T(2,128)}, u32[]{:S(2)}) copy-start(f32[2,256]{1,0:T(2,128)} %param.9) | copy-start | bytes 6148
  237.0 413.9 %all-reduce.5.cloned.1.call-start = ((), (), s32[]{:S(2)}) async-start(), calls=%async_computation.3 | async-start | bytes 524288 | tf_op jit(solution)/shard_map/psum | solution.py:56
Sparse Core Ops, SparseCore 0:
  10.0 140.8 all-gather.2
  154.0 56.1 all-gather.4
  237.1 144.7 all-reduce.2
  384.9 265.9 all-reduce.4
